TPU v7x, 256 devices: a whole 4x4x8 slice. The times are simulated.
256 devices in a mesh: dp: 16 (over x, z_lo), shard: 16 (over z_hi, y, core).
Axes of the slice: x: 4, y: 4, z: 8 (z_hi: 2, z_lo: 4; z = z_hi * 4 + z_lo), core: 2. Of those that a mesh axis runs over, the one named last changes fastest.
Arguments:
- codes: int32 [16, 5, 8, 64], P('dp', None, None, 'shard'), may hold values from 0 to 262143
- lengths: int32 [16], P('dp'), may hold values from 1 to 5, 48 in all
- hidden: bfloat16 [16, 5, 8, 64, 512], P('dp', None, None, 'shard'), may hold values from -6 to 6
- embed: bfloat16 [18, 512], replicated, may hold values from -1.5 to 1.5
- conv_weight: bfloat16 [512, 27, 512], P('shard'), may hold values from -0.0546875 to 0.0546875
- gain: float32 [512], replicated, may hold values from 0.1 to 1.9
- bias: float32 [512], replicated, may hold values from -3 to 3
- cotangent: bfloat16 [16, 5, 16, 128, 128], P('dp', None, None, 'shard'), may hold values from -6 to 6
Outputs:
- decoded: bfloat16 [16, 5, 16, 128, 128], P('dp', None, None, 'shard')
- grad_hidden: bfloat16 [16, 5, 8, 64, 512], P('dp', None, None, 'shard')
- grad_conv: float32 [512, 27, 512], P('shard')
- grad_embed: float32 [18, 512], replicated
- grad_gain: float32 [512], replicated
- grad_bias: float32 [512], replicated
Inputs may be any that keep to these rules, and one draw needn't show every extreme that they name: Frames from lengths[c] on are padding; some clip has all 5 frames valid.
All inputs are finite; a program needn't handle non-finite values. No bound on the sum of `lengths` on one device may be relied on, other than what follows from the above.
Results may differ from a plain program's by a relative error of at most 0.02.
Values may be sent and summed in bfloat16 or wider, within the bound.
A program may use at most 128 MiB of HBM per device.

v0:
```python
import jax
import jax.numpy as jnp
from jax import lax
from jax.sharding import PartitionSpec as P

CODE_BITS = 18
GROUPS = 32
eps_norm = 1e-05


def forward_taps(padded, frames, height, width):
    taps = []
    for depth_tap in range(3):
        for row_tap in range(3):
            for col_tap in range(3):
                taps.append(
                    padded[
                        depth_tap : depth_tap + frames,
                        row_tap : row_tap + height,
                        col_tap : col_tap + width,
                    ]
                )
    return taps


def backward_taps(padded, frames, height, width):
    taps = []
    for depth_tap in range(3):
        for row_tap in range(3):
            for col_tap in range(3):
                taps.append(
                    padded[
                        2 - depth_tap : 2 - depth_tap + frames,
                        2 - row_tap : 2 - row_tap + height,
                        2 - col_tap : 2 - col_tap + width,
                    ]
                )
    return taps


def slab_columns(spread, frames, height, slab_width):
    padded = jnp.pad(spread, ((2, 0), (1, 1), (1, 1), (0, 0)))
    return jnp.concatenate(forward_taps(padded, frames, height, slab_width), axis=3)


def on_device(codes, lengths, hidden, embed, conv_weight, gain, bias, cotangent):
    frames = codes.shape[1]
    height = codes.shape[2]
    width = codes.shape[3]
    share = conv_weight.shape[0]
    channels = conv_weight.shape[2]
    quarter = channels // 4
    shards = lax.axis_size("shard")
    slab_width = width * shards
    positions = frames * height * width
    groups = GROUPS
    per_group = channels // groups
    frame_mask = (jnp.arange(frames) < lengths[0]).astype(jnp.float32)
    mask_cells = frame_mask[:, None, None, None]
    mask_groups = frame_mask[:, None, None, None, None]
    powers = 2 ** jnp.arange(CODE_BITS, dtype=jnp.int32)
    bits = (codes[0][..., None] // powers % 2 * 2 - 1).astype(jnp.bfloat16)
    embedded = jnp.dot(
        bits.reshape(positions, CODE_BITS), embed, preferred_element_type=jnp.float32
    ).reshape(frames, height, width, channels)
    features = ((embedded + hidden[0].astype(jnp.float32)) * mask_cells).astype(jnp.bfloat16)
    spread = lax.all_to_all(features, "shard", split_axis=3, concat_axis=2, tiled=True)
    slab_patches = slab_columns(spread, frames, height, slab_width)
    flat_share = jnp.transpose(conv_weight, (1, 0, 2)).reshape(27 * share, channels)
    part_sums = jnp.dot(
        slab_patches.reshape(-1, 27 * share), flat_share, preferred_element_type=jnp.float32
    ).reshape(frames, height, slab_width, channels)
    conv_out = lax.psum_scatter(
        part_sums.astype(jnp.bfloat16), "shard", scatter_dimension=2, tiled=True
    ).astype(jnp.float32)
    grouped = conv_out.reshape(frames, height, width, groups, per_group)
    sum_one, sum_two = lax.psum(
        (
            jnp.sum(grouped * mask_groups, axis=(0, 1, 2, 4)),
            jnp.sum(grouped * grouped * mask_groups, axis=(0, 1, 2, 4)),
        ),
        "shard",
    )
    count = lengths[0].astype(jnp.float32) * (height * width * shards * per_group)
    mean = sum_one / count
    variance = sum_two / count - mean * mean
    inv_std = lax.rsqrt(variance + eps_norm)
    gain_group = gain.reshape(groups, per_group)
    bias_group = bias.reshape(groups, per_group)
    normed = (grouped - mean[:, None]) * inv_std[:, None]
    pre = normed * gain_group + bias_group
    sigma = jax.nn.sigmoid(pre)
    activated = pre * sigma * mask_groups
    decoded = (
        activated.reshape(frames, height, width, 2, 2, quarter)
        .transpose(0, 1, 3, 2, 4, 5)
        .reshape(frames, 2 * height, 2 * width, quarter)
        .astype(jnp.bfloat16)[None]
    )
    upstream = (
        cotangent[0]
        .astype(jnp.float32)
        .reshape(frames, height, 2, width, 2, quarter)
        .transpose(0, 1, 3, 2, 4, 5)
        .reshape(frames, height, width, groups, per_group)
        * mask_groups
    )
    d_pre = upstream * sigma * (1.0 + pre * (1.0 - sigma))
    gain_term = jnp.sum(d_pre * normed, axis=(0, 1, 2)).reshape(channels)
    bias_term = jnp.sum(d_pre, axis=(0, 1, 2)).reshape(channels)
    d_norm = d_pre * gain_group
    tot_one, tot_two = lax.psum(
        (jnp.sum(d_norm, axis=(0, 1, 2, 4)), jnp.sum(d_norm * normed, axis=(0, 1, 2, 4))), "shard"
    )
    d_conv = (
        (
            inv_std[:, None]
            * (d_norm - tot_one[:, None] / count - normed * tot_two[:, None] / count)
            * mask_groups
        )
        .reshape(frames, height, width, channels)
        .astype(jnp.bfloat16)
    )
    whole_grad = lax.all_gather(d_conv, "shard", axis=2, tiled=True)
    back_share = jnp.transpose(conv_weight, (2, 1, 0)).reshape(channels, 27 * share)
    tap_images = jnp.dot(
        whole_grad.reshape(-1, channels), back_share, preferred_element_type=jnp.float32
    ).reshape(frames, height, slab_width, 27 * share)
    padded_images = jnp.pad(tap_images, ((0, 2), (1, 1), (1, 1), (0, 0)))
    input_sum = jnp.zeros((frames, height, slab_width, share), jnp.float32)
    for tap_index, shifted in enumerate(backward_taps(padded_images, frames, height, slab_width)):
        input_sum = input_sum + shifted[..., tap_index * share : (tap_index + 1) * share]
    d_features = lax.all_to_all(
        input_sum.astype(jnp.bfloat16), "shard", split_axis=2, concat_axis=3, tiled=True
    )
    clip_part = jnp.einsum(
        "pk,pc->kc",
        slab_patches.reshape(-1, 27 * share),
        whole_grad.reshape(-1, channels),
        preferred_element_type=jnp.float32,
    )
    weight_sum = clip_part.reshape(27, share, channels).transpose(1, 0, 2)
    grad_conv = lax.psum(weight_sum.astype(jnp.bfloat16), "dp").astype(jnp.float32)
    grad_hidden = d_features * mask_cells.astype(jnp.bfloat16)
    embed_term = jnp.dot(
        bits.reshape(positions, CODE_BITS).T,
        grad_hidden.reshape(positions, channels),
        preferred_element_type=jnp.float32,
    )
    grad_embed, grad_gain, grad_bias = lax.psum((embed_term, gain_term, bias_term), ("dp", "shard"))
    return (decoded, grad_hidden[None], grad_conv, grad_embed, grad_gain, grad_bias)


def solution(mesh):
    return jax.shard_map(
        on_device,
        mesh=mesh,
        in_specs=(
            P("dp", None, None, "shard"),
            P("dp"),
            P("dp", None, None, "shard", None),
            P(),
            P("shard", None, None),
            P(),
            P(),
            P("dp", None, None, "shard", None),
        ),
        out_specs=(
            P("dp", None, None, "shard", None),
            P("dp", None, None, "shard", None),
            P("shard", None, None),
            P(),
            P(),
            P(),
        ),
        check_vma=False,
    )
```

profile of v0, /device:TPU:8, one launch (start us, length us, event | category | flops | bytes accessed | tf_op | source)
XLA Modules:
  0.0 610.6 jit_solution(5969993515602103230)
XLA Ops:
  8.7 2.7 fusion.29
  14.0 3.4 reshape.359
  17.4 20.4 %all_to_all.39 = bf16[16,2,2560]{2,1,0:T(2,128)(2,1)S(1)} all-to-all(bf16[16,2,2560]{2,1,0:T(2,128)(2,1)} %reshape.359), channel_id=1, replica_groups=mesh['dp'=16,'shard'=16] {'shard'}, dimensions={0} | all-to-all | bytes 327680 | tf_op jit(solution)/shard_map/all_to_all | solution.py:67
  37.8 4.1 reshape.360
  41.9 4.3 copy.35
  46.3 2.9 pad_slice_fusion.27
  49.2 6.8 %pad_slice_fusion.26 = (bf16[5,8,64,32]{3,2,1,0:T(8,128)(2,1)S(1)}, bf16[5,8,64,32]{3,2,1,0:T(8,128)(2,1)S(1)}, bf16[5,8,64,32]{3,2,1,0:T(8,128)(2,1)S(1)}, bf16...) fusion(bf16[5,8,64,32]{3,2,1,0:T(8,128)(2,1)S(1)} %bitcast.128), kind=kLoop, calls=%fused_computation.26 | loop fusion | bytes 3276800 | tf_op jit(solution)/shard_map/slice | solution.py:17
  56.0 16.7 %concatenate.61 = bf16[5,8,64,864]{3,2,1,0:T(8,128)(2,1)} concatenate(bf16[5,8,64,32]{3,2,1,0:T(8,128)(2,1)} %get-tuple-element.46, bf16[5,8,64,32]{3,2,1,0:T(8,128)(2,1)S(1)} %get-tuple-element.22, bf16[5,8,64,32]{3,2,1,0:T(8,128)(2,1)S(1)} %get-tuple-element.23, bf16[5,8,64,32]{3,2,1,0:T(8,128)(2,1)} %get-tuple-element.24, bf16[5,8,64,32]{3,2,1,0:T(8,128)(2,1)} %get-tuple-element.25, ...), dimensions={3} | concatenate | bytes 8847360 | tf_op jit(solution)/shard_map/concatenate | solution.py:43
  72.7 5.4 convolution_convert_fusion
  78.1 3.0 copy.36
  85.9 172.9 %all-reduce.11.cloned.1.call-done = bf16[5,8,64,512]{3,1,2,0:T(8,128)(2,1)} async-done(((bf16[5,8,64,512]{3,1,2,0:T(8,128)(2,1)}), bf16[5,8,64,512]{3,1,2,0:T(8,128)(2,1)}) %all-reduce.11.cloned.1.call-update) | async-done | bytes 2621456
  262.1 50.1 %all-reduce.5 = (f32[32]{0:T(128)S(1)}, f32[32]{0:T(128)S(1)}) all-reduce(f32[32]{0:T(128)S(1)} %reduce_sum.67, f32[32]{0:T(128)} %reduce_sum.73), channel_id=1, replica_groups=mesh['dp'=16,'shard'=16] {'shard'}, use_global_device_ids=true, to_apply=%region_3.4 | all-reduce | flops 64 | bytes 512 | tf_op jit(solution)/shard_map/psum | solution.py:77
  320.4 42.9 %all-reduce.4 = (f32[32]{0:T(128)S(1)}, f32[32]{0:T(128)S(1)}) all-reduce(f32[32]{0:T(128)S(1)} %reduce_sum.93, f32[32]{0:T(128)} %reduce_sum.90), channel_id=1, replica_groups=mesh['dp'=16,'shard'=16] {'shard'}, use_global_device_ids=true, to_apply=%region_12.13 | all-reduce | flops 64 | bytes 512 | tf_op jit(solution)/shard_map/psum | solution.py:112
  365.6 16.7 %concatenate.89 = bf16[2560,864]{1,0:T(8,128)(2,1)} concatenate(bf16[2560,32]{1,0:T(8,128)(2,1)} %bitcast.158, bf16[2560,32]{1,0:T(8,128)(2,1)S(1)} %bitcast.134, bf16[2560,32]{1,0:T(8,128)(2,1)S(1)} %bitcast.135, bf16[2560,32]{1,0:T(8,128)(2,1)} %bitcast.136, bf16[2560,32]{1,0:T(8,128)(2,1)} %bitcast.137, bf16[2560,32]{1,0:T(8,128)(2,1)} %bitcast.138, ...), dimensions={1} | concatenate | bytes 8847360 | tf_op jit(solution)/shard_map/concatenate | solution.py:43
  382.4 7.3 %copy.42 = bf16[864,2560]{1,0:T(8,128)(2,1)} copy(bf16[864,2560]{0,1:T(8,128)(2,1)} %bitcast.126) | data formatting | bytes 8847360 | tf_op jit(solution)/shard_map/pk,pc->kc/dot_general | solution.py:136
  389.6 43.9 %all-gather.2.cloned.1.call-done = bf16[5,8,64,512]{3,1,2,0:T(8,128)(2,1)} async-done(((bf16[5,8,4,512]{3,1,2,0:T(8,128)(2,1)}), bf16[5,8,64,512]{3,1,2,0:T(8,128)(2,1)}) %all-gather.2.cloned.1.call-update) | async-done | bytes 2621456 | tf_op jit(solution)/shard_map/all_gather | solution.py:124
  433.6 2.8 copy.39
  436.6 3.4 fusion
  440.0 3.1 fusion.55
  443.1 6.2 %fusion.27 = bf16[5,8,64,32]{3,2,1,0:T(8,128)(2,1)S(1)} fusion(f32[5,8,64,864]{3,2,1,0:T(8,128)S(1)} %fusion.55), kind=kLoop, calls=%fused_computation.81 | loop fusion | flops 2211840 | bytes 10649600 | tf_op jit(solution)/shard_map/convert_element_type | solution.py:134
  450.9 4.5 all-to-all-start.1
  456.2 8.4 %all-to-all-done.1 = bf16[16,2,2560]{2,1,0:T(2,128)(2,1)S(1)} async-done(((bf16[16,2,2560]{2,1,0:T(2,128)(2,1)}), bf16[16,2,2560]{2,1,0:T(2,128)(2,1)S(1)}, u32[]{:S(2)}, u32[]{:S(2)}) %all-to-all-start.1) | async-done | bytes 163872 | tf_op jit(solution)/shard_map/all_to_all | solution.py:133
  467.8 79.0 %all-reduce.3 = (f32[18,512]{1,0:T(8,128)}, f32[512]{0:T(512)}, f32[512]{0:T(512)}) all-reduce(f32[18,512]{1,0:T(8,128)S(1)} %convolution_bitcast_fusion, f32[512]{0:T(512)S(1)} %bitcast.175, f32[512]{0:T(512)S(1)} %bitcast.176), channel_id=1, replica_groups=mesh['dp'=16,'shard'=16] {'dp','shard'}, use_global_device_ids=true, to_apply=%region_14.15 | all-reduce | flops 10240 | bytes 81920 | tf_op jit(solution)/shard_map/psum | solution.py:150
  547.6 53.8 %all-reduce.9.cloned.1.call-done = bf16[32,27,512]{2,0,1:T(8,128)(2,1)} async-done(((bf16[32,27,512]{2,0,1:T(8,128)(2,1)}), bf16[32,27,512]{2,0,1:T(8,128)(2,1)}) %all-reduce.9.cloned.1.call-update) | async-done | bytes 884752 | tf_op jit(solution)/shard_map/psum | solution.py:143
  (86 shorter events, 30.3 us)
Async XLA Ops:
  7.2 65.5 %copy-start = (bf16[32,27,512]{2,0,1:T(8,128)(2,1)S(1)}, bf16[32,27,512]{2,0,1:T(8,128)(2,1)}, u32[]{:S(2)}) copy-start(bf16[32,27,512]{2,0,1:T(8,128)(2,1)} %param.12) | copy-start | bytes 2654212
  7.2 251.7 %all-reduce.11.cloned.1.call-start = ((), (), s32[]{:S(2)}) async-start(), calls=%async_computation.4 | async-start | bytes 5242880
  7.2 6.7 %copy-start.12 = (s32[18]{0:T(128)}, s32[18]{0:T(128)S(1)}, u32[]{:S(2)}) copy-start(s32[18]{0:T(128)S(1)} %get-tuple-element.49) | copy-start | bytes 220
  7.3 6.7 %copy-start.14 = (s32[18]{0:T(128)}, s32[18]{0:T(128)S(1)}, u32[]{:S(2)}) copy-start(s32[18]{0:T(128)S(1)} %get-tuple-element.50) | copy-start | bytes 220
  8.0 250.9 %copy-start.9 = (f32[5]{0:T(128)}, f32[5]{0:T(128)S(1)}, u32[]{:S(2)}) copy-start(f32[5]{0:T(128)S(1)} %compare_convert_fusion) | copy-start | bytes 64
  81.1 3.6 copy-start.11
  81.1 234.4 %copy-start.4 = (f32[512]{0:T(512)S(1)}, f32[512]{0:T(512)}, u32[]{:S(2)}) copy-start(f32[512]{0:T(512)} %param.13) | copy-start | bytes 6148
  81.2 352.4 %all-gather.2.cloned.1.call-start = ((), (), s32[]{:S(2)}) async-start(), calls=%async_computation.2 | async-start | bytes 2785280 | tf_op jit(solution)/shard_map/all_gather | solution.py:124
  312.1 0.5 copy-start.10
  312.7 50.9 %copy-start.6 = (f32[512]{0:T(512)S(1)}, f32[512]{0:T(512)}, u32[]{:S(2)}) copy-start(f32[512]{0:T(512)} %param.14) | copy-start | bytes 6148
  365.6 235.9 %all-reduce.9.cloned.1.call-start = ((), (), s32[]{:S(2)}) async-start(), calls=%async_computation.3 | async-start | bytes 1769472 | tf_op jit(solution)/shard_map/psum | solution.py:143
  433.6 3.0 copy-start.1
  436.6 3.4 copy-start.2
  449.3 6.1 %copy-start.3 = (bf16[5,8,2,4,2,128]{5,1,4,2,3,0:T(8,128)(2,1)S(1)}, bf16[5,8,2,4,2,128]{5,1,4,2,3,0:T(8,128)(2,1)}, u32[]{:S(2)}) copy-start(bf16[5,8,2,4,2,128]{5,1,4,2,3,0:T(8,128)(2,1)} %get-tuple-element.48) | copy-start | bytes 491524
  450.9 13.8 %all-to-all-start.1 = ((bf16[16,2,2560]{2,1,0:T(2,128)(2,1)}), bf16[16,2,2560]{2,1,0:T(2,128)(2,1)S(1)}, u32[]{:S(2)}, u32[]{:S(2)}) async-start(bf16[16,2,2560]{2,1,0:T(2,128)(2,1)} %reshape.361), calls=%async_computation.1 | async-start | bytes 327680 | tf_op jit(solution)/shard_map/all_to_all | solution.py:133
  465.3 1.4 copy-start.5
  465.3 1.4 copy-start.13
  465.3 1.4 copy-start.15
  465.6 2.2 copy-start.7
  465.6 2.2 copy-start.8
Sparse Core Ops, SparseCore 0:
  81.3 177.5 all-reduce.10
  365.7 67.8 all-gather.1
  440.1 161.2 all-reduce.8
where the time goes:
time: 615 us; the launch traced here: 611 us
  waiting for transfers between devices  279 us (45%)
  blocking collectives  192 us (31%)
  local copies, waits for them, and re-layouts  82.7 us (13%)
  other arithmetic  20.8 us (3%)
  matrix products  15.5 us (3%)
  between operations  15.4 us (3%)
    unnamed x4, waiting for transfers between devices  173 us
    psum x1, blocking collectives, on_device(): lax.psum((embed_term, gain_term, bias_term), ('dp', 'shard'))  79 us
    psum x1, waiting for transfers between devices, on_device(): lax.psum(weight_sum.astype(jnp.bfloat16), 'dp').astype(jnp.float32)  53.8 us
    psum x1, blocking collectives, on_device(): lax.psum((jnp.sum(grouped * mask_groups, axis=(0, 1, 2, 4)), jnp.sum(grou...  50.1 us
    all_gather x1, waiting for transfers between devices, on_device(): whole_grad = lax.all_gather(d_conv, 'shard', axis=2, tiled=True)  43.9 us
    psum x1, blocking collectives, on_device(): lax.psum((jnp.sum(d_norm, axis=(0, 1, 2, 4)), jnp.sum(d_norm * normed, ax...  42.9 us
    concatenate x2, local copies, waits for them, and re-layouts, slab_columns(): jnp.concatenate(forward_taps(padded, frames, height, slab_width), axis=3)  33.4 us
    all_to_all x1, blocking collectives, on_device(): lax.all_to_all(features, 'shard', split_axis=3, concat_axis=2, tiled=True)  20.4 us
  transfers between devices with their start and end apart: 4, of which 4 were waited for; matrix products, arithmetic and copies ran while one was open for 7% of the time, Pallas kernels for 0%

commit v1 on v0

--- a/solution.py
+++ b/solution.py
@@ -140,7 +140,9 @@
         preferred_element_type=jnp.float32,
     )
     weight_sum = clip_part.reshape(27, share, channels).transpose(1, 0, 2)
-    grad_conv = lax.psum(weight_sum.astype(jnp.bfloat16), "dp").astype(jnp.float32)
+    grad_conv = jnp.sum(lax.all_gather(weight_sum.astype(jnp.bfloat16), "dp"), axis=0).astype(
+        jnp.float32
+    )
     grad_hidden = d_features * mask_cells.astype(jnp.bfloat16)
     embed_term = jnp.dot(
         bits.reshape(positions, CODE_BITS).T,

time: 615 us -> 765 us (1.24)
  waiting for transfers between devices: 279 us -> 411 us
  blocking collectives: 192 us -> 203 us
    all_gather x0 -> x1, waiting for transfers between devices: none -> 184 us  [on_device(): lax.all_gather(weight_sum.astype(jnp.bfloat16), 'dp')]
    psum x1 -> x0, waiting for transfers between devices: 53.8 us -> none  [on_device(): lax.psum(weight_sum.astype(jnp.bfloat16), 'dp').astype(jnp.float32)]
    psum x1, blocking collectives: 79 us -> 89.6 us  [on_device(): lax.psum((embed_term, gain_term, bias_term), ('dp', 'shard'))]
    reduce_sum x0 -> x1, other arithmetic: none -> 8.33 us  [on_device(): jnp.sum(lax.all_gather(weight_sum.astype(jnp.bfloat16), 'dp'), axis=0)]
  transfers between devices with their start and end apart: 4 -> 4, of which waited for: 4 -> 4; matrix products, arithmetic and copies ran while one was open for 7% -> 6% of each run, Pallas kernels for 0% -> 0%
where the time goes in v1:
time: 765 us; the launch traced here: 760 us
  waiting for transfers between devices  411 us (54%)
  blocking collectives  203 us (27%)
  local copies, waits for them, and re-layouts  82.8 us (11%)
  other arithmetic  27.9 us (4%)
  matrix products  15.5 us (2%)
  between operations  15.4 us (2%)
    all_gather x1, waiting for transfers between devices, on_device(): lax.all_gather(weight_sum.astype(jnp.bfloat16), 'dp')  184 us
    unnamed x4, waiting for transfers between devices  173 us
    psum x1, blocking collectives, on_device(): lax.psum((embed_term, gain_term, bias_term), ('dp', 'shard'))  89.6 us
    psum x1, blocking collectives, on_device(): lax.psum((jnp.sum(grouped * mask_groups, axis=(0, 1, 2, 4)), jnp.sum(grou...  50.1 us
    all_gather x1, waiting for transfers between devices, on_device(): whole_grad = lax.all_gather(d_conv, 'shard', axis=2, tiled=True)  43.9 us
    psum x1, blocking collectives, on_device(): lax.psum((jnp.sum(d_norm, axis=(0, 1, 2, 4)), jnp.sum(d_norm * normed, ax...  42.9 us
    concatenate x2, local copies, waits for them, and re-layouts, slab_columns(): jnp.concatenate(forward_taps(padded, frames, height, slab_width), axis=3)  33.4 us
    all_to_all x1, blocking collectives, on_device(): lax.all_to_all(features, 'shard', split_axis=3, concat_axis=2, tiled=True)  20.4 us
  transfers between devices with their start and end apart: 4, of which 4 were waited for; matrix products, arithmetic and copies ran while one was open for 6% of the time, Pallas kernels for 0%

profile of v1, /device:TPU:8, one launch (start us, length us, event | category | flops | bytes accessed | tf_op | source)
XLA Modules:
  0.0 760.1 jit_solution(238833943727757489)
XLA Ops:
  14.0 3.4 reshape.360
  17.4 20.4 %all_to_all.39 = bf16[16,2,2560]{2,1,0:T(2,128)(2,1)S(1)} all-to-all(bf16[16,2,2560]{2,1,0:T(2,128)(2,1)} %reshape.360), channel_id=1, replica_groups=mesh['dp'=16,'shard'=16] {'shard'}, dimensions={0} | all-to-all | bytes 327680 | tf_op jit(solution)/shard_map/all_to_all | solution.py:67
  37.8 4.1 reshape.361
  41.9 4.3 copy.35
  46.3 2.9 pad_slice_fusion.27
  49.2 6.9 pad_slice_fusion.26
  56.1 16.7 %concatenate.61 = bf16[5,8,64,864]{3,2,1,0:T(8,128)(2,1)} concatenate(bf16[5,8,64,32]{3,2,1,0:T(8,128)(2,1)} %get-tuple-element.46, bf16[5,8,64,32]{3,2,1,0:T(8,128)(2,1)S(1)} %get-tuple-element.22, bf16[5,8,64,32]{3,2,1,0:T(8,128)(2,1)S(1)} %get-tuple-element.23, bf16[5,8,64,32]{3,2,1,0:T(8,128)(2,1)} %get-tuple-element.24, bf16[5,8,64,32]{3,2,1,0:T(8,128)(2,1)} %get-tuple-element.25, ...), dimensions={3} | concatenate | bytes 8847360 | tf_op jit(solution)/shard_map/concatenate | solution.py:43
  72.8 5.4 convolution_convert_fusion
  78.2 3.0 copy.36
  86.0 173.0 %all-reduce.8.cloned.1.call-done = bf16[5,8,64,512]{3,1,2,0:T(8,128)(2,1)} async-done(((bf16[5,8,64,512]{3,1,2,0:T(8,128)(2,1)}), bf16[5,8,64,512]{3,1,2,0:T(8,128)(2,1)}) %all-reduce.8.cloned.1.call-update) | async-done | bytes 2621456
  262.2 50.1 %all-reduce.5 = (f32[32]{0:T(128)S(1)}, f32[32]{0:T(128)S(1)}) all-reduce(f32[32]{0:T(128)S(1)} %reduce_sum.96, f32[32]{0:T(128)} %reduce_sum.99), channel_id=1, replica_groups=mesh['dp'=16,'shard'=16] {'shard'}, use_global_device_ids=true, to_apply=%region_3.4 | all-reduce | flops 64 | bytes 512 | tf_op jit(solution)/shard_map/psum | solution.py:77
  320.5 42.9 %all-reduce.4 = (f32[32]{0:T(128)S(1)}, f32[32]{0:T(128)S(1)}) all-reduce(f32[32]{0:T(128)S(1)} %reduce_sum.105, f32[32]{0:T(128)} %reduce_sum.102), channel_id=1, replica_groups=mesh['dp'=16,'shard'=16] {'shard'}, use_global_device_ids=true, to_apply=%region_12.13 | all-reduce | flops 64 | bytes 512 | tf_op jit(solution)/shard_map/psum | solution.py:112
  365.8 16.7 %concatenate.89 = bf16[2560,864]{1,0:T(8,128)(2,1)} concatenate(bf16[2560,32]{1,0:T(8,128)(2,1)} %bitcast.160, bf16[2560,32]{1,0:T(8,128)(2,1)S(1)} %bitcast.136, bf16[2560,32]{1,0:T(8,128)(2,1)S(1)} %bitcast.137, bf16[2560,32]{1,0:T(8,128)(2,1)} %bitcast.138, bf16[2560,32]{1,0:T(8,128)(2,1)} %bitcast.139, bf16[2560,32]{1,0:T(8,128)(2,1)} %bitcast.140, ...), dimensions={1} | concatenate | bytes 8847360 | tf_op jit(solution)/shard_map/concatenate | solution.py:43
  382.5 7.3 copy.42
  389.7 43.9 %all-gather.4.cloned.1.call-done = bf16[5,8,64,512]{3,1,2,0:T(8,128)(2,1)} async-done(((bf16[5,8,4,512]{3,1,2,0:T(8,128)(2,1)}), bf16[5,8,64,512]{3,1,2,0:T(8,128)(2,1)}) %all-gather.4.cloned.1.call-update) | async-done | bytes 2621456 | tf_op jit(solution)/shard_map/all_gather | solution.py:124
  433.7 2.8 copy.39
  436.7 3.4 fusion
  440.1 3.1 fusion.55
  443.2 6.2 fusion.27
  451.0 4.5 all-to-all-start.1
  456.4 9.7 %all-to-all-done.1 = bf16[16,2,2560]{2,1,0:T(2,128)(2,1)S(1)} async-done(((bf16[16,2,2560]{2,1,0:T(2,128)(2,1)}), bf16[16,2,2560]{2,1,0:T(2,128)(2,1)S(1)}, u32[]{:S(2)}, u32[]{:S(2)}) %all-to-all-start.1) | async-done | bytes 163872 | tf_op jit(solution)/shard_map/all_to_all | solution.py:133
  469.1 89.6 %all-reduce.3 = (f32[18,512]{1,0:T(8,128)}, f32[512]{0:T(512)}, f32[512]{0:T(512)}) all-reduce(f32[18,512]{1,0:T(8,128)S(1)} %convolution_bitcast_fusion, f32[512]{0:T(512)S(1)} %bitcast.177, f32[512]{0:T(512)S(1)} %bitcast.178), channel_id=1, replica_groups=mesh['dp'=16,'shard'=16] {'dp','shard'}, use_global_device_ids=true, to_apply=%region_14.15 | all-reduce | flops 10240 | bytes 81920 | tf_op jit(solution)/shard_map/psum | solution.py:152
  559.6 184.2 %all-gather.6.cloned.1.call-done = bf16[512,27,512]{2,0,1:T(8,128)(2,1)} async-done(((bf16[32,27,512]{2,0,1:T(8,128)(2,1)}), bf16[512,27,512]{2,0,1:T(8,128)(2,1)}) %all-gather.6.cloned.1.call-update) | async-done | bytes 14155792 | tf_op jit(solution)/shard_map/all_gather | solution.py:143
  743.8 8.3 %reduce_sum.106 = bf16[32,27,512]{2,0,1:T(8,128)(2,1)S(1)} reduce(bf16[16,32,27,512]{3,1,0,2:T(8,128)(2,1)} %bitcast.132, bf16[]{:T(256)} %constant.52.clone.1), dimensions={0}, to_apply=%region_13.14 | reduce | flops 6635520 | bytes 15040514 | tf_op jit(solution)/shard_map/reduce_sum | solution.py:143
  (87 shorter events, 31.8 us)
Async XLA Ops:
  7.2 65.6 %copy-start = (bf16[32,27,512]{2,0,1:T(8,128)(2,1)S(1)}, bf16[32,27,512]{2,0,1:T(8,128)(2,1)}, u32[]{:S(2)}) copy-start(bf16[32,27,512]{2,0,1:T(8,128)(2,1)} %param.12) | copy-start | bytes 2654212
  7.2 251.8 %all-reduce.8.cloned.1.call-start = ((), (), s32[]{:S(2)}) async-start(), calls=%async_computation.4 | async-start | bytes 5242880
  7.2 6.7 copy-start.12
  7.3 6.7 copy-start.14
  8.0 251.0 %copy-start.9 = (f32[5]{0:T(128)}, f32[5]{0:T(128)S(1)}, u32[]{:S(2)}) copy-start(f32[5]{0:T(128)S(1)} %compare_convert_fusion) | copy-start | bytes 64
  81.2 3.6 copy-start.11
  81.2 234.4 %copy-start.4 = (f32[512]{0:T(512)S(1)}, f32[512]{0:T(512)}, u32[]{:S(2)}) copy-start(f32[512]{0:T(512)} %param.13) | copy-start | bytes 6148
  81.2 352.4 %all-gather.4.cloned.1.call-start = ((), (), s32[]{:S(2)}) async-start(), calls=%async_computation.2 | async-start | bytes 2785280 | tf_op jit(solution)/shard_map/all_gather | solution.py:124
  312.2 0.5 copy-start.10
  312.8 50.9 %copy-start.6 = (f32[512]{0:T(512)S(1)}, f32[512]{0:T(512)}, u32[]{:S(2)}) copy-start(f32[512]{0:T(512)} %param.14) | copy-start | bytes 6148
  365.7 378.1 %all-gather.6.cloned.1.call-start = ((), (), s32[]{:S(2)}) async-start(), calls=%async_computation.3 | async-start | bytes 15040512 | tf_op jit(solution)/shard_map/all_gather | solution.py:143
  433.7 3.0 copy-start.1
  436.7 3.4 copy-start.2
  449.4 6.1 copy-start.3
  451.0 15.0 %all-to-all-start.1 = ((bf16[16,2,2560]{2,1,0:T(2,128)(2,1)}), bf16[16,2,2560]{2,1,0:T(2,128)(2,1)S(1)}, u32[]{:S(2)}, u32[]{:S(2)}) async-start(bf16[16,2,2560]{2,1,0:T(2,128)(2,1)} %reshape.362), calls=%async_computation.1 | async-start | bytes 327680 | tf_op jit(solution)/shard_map/all_to_all | solution.py:133
  466.6 1.4 copy-start.5
  466.6 1.4 copy-start.13
  466.6 1.4 copy-start.15
  466.9 2.2 copy-start.7
  466.9 2.2 copy-start.8
Sparse Core Ops, SparseCore 0:
  81.3 177.5 all-reduce.7
  365.8 67.8 all-gather.3
  440.2 303.5 all-gather.5
